TPU v7x, 512 devices: a whole 4x8x8 slice. The times are simulated.
512 devices in a mesh: lon: 32 (over z_lo, y), lat: 16 (over z_hi, x, core).
Axes of the slice: x: 4, y: 8, z: 8 (z_hi: 2, z_lo: 4; z = z_hi * 4 + z_lo), core: 2. Of those that a mesh axis runs over, the one named last changes fastest.
Arguments:
- wind_u: float32 [720, 1440, 16], P('lat', 'lon'), may hold values from -6 to 6
- wind_v: float32 [720, 1440, 16], P('lat', 'lon'), may hold values from -6 to 6
- vorticity: float32 [720, 1440, 16], P('lat', 'lon'), may hold values from -6 to 6
- sample_level: int32 [16], replicated, may hold values from 0 to 1, as said below
- slot_wavenumber: int32 [736], P('lon'), may hold values from -1 to 719, as said below
- legendre_p: bfloat16 [720, 529920], P('lat', 'lon'), may hold values from -5 to 5
- legendre_h: bfloat16 [720, 529920], P('lat', 'lon'), may hold values from -5 to 5
Outputs:
- spectra: float32 [2, 529920], P(None, ('lon', 'lat'))
Inputs may be any that keep to these rules, and one draw needn't show every extreme that they name: `sample_level`: each level is named by exactly 8 samples. `slot_wavenumber`: each wavenumber from 0 to 719 stands in exactly one slot; the remaining slots hold -1.
All inputs are finite; a program needn't handle non-finite values.
Results may differ from a plain program's by a relative error of at most 0.0014.
Values sent between devices are 32-bit elements; how exact they have to be, the bound alone decides.
A program may use at most 128 MiB of HBM per device.

v0:
```python
import math
import jax
import jax.numpy as jnp
from jax import lax
from jax.sharding import PartitionSpec as P

NLON = 1440
NLAT = 720
MAXM = 720
LEV = 2
DAYS = 8
S = 16


def remove_means(field, onehot):
    means = jnp.einsum("jis,sl->jil", field, onehot, precision=lax.Precision.HIGHEST) / DAYS
    return field - jnp.einsum("jil,sl->jis", means, onehot, precision=lax.Precision.HIGHEST)


def fourier_table(waves, count):
    longitude = jnp.arange(count, dtype=jnp.int32)
    present = waves >= 0
    clipped = jnp.maximum(waves, 0)
    residue = longitude[:, None] * clipped[None, :] % NLON
    angle = residue.astype(jnp.float32) * (2.0 * math.pi / NLON)
    weight = present.astype(jnp.float32)[None, :] / NLON
    return jnp.stack([jnp.cos(angle) * weight, jnp.sin(angle) * weight], axis=2)


def body(wind_u, wind_v, vorticity, sample_level, slot_wavenumber, legendre_p, legendre_h):
    band_rows = wind_u.shape[0]
    lat_count = lax.axis_size("lat")
    onehot = (sample_level[:, None] == jnp.arange(LEV, dtype=jnp.int32)[None, :]).astype(
        jnp.float32
    )
    eddy_u = remove_means(wind_u, onehot)
    eddy_v = remove_means(wind_v, onehot)
    eddy_z = remove_means(vorticity, onehot)
    row_index = lax.axis_index("lat") * band_rows + jnp.arange(band_rows, dtype=jnp.int32)
    latitude = (row_index.astype(jnp.float32) + 0.5) * (math.pi / NLAT) - 0.5 * math.pi
    cosine = jnp.cos(latitude)[:, None, None]
    fluxes = jnp.concatenate([eddy_u * eddy_z * cosine, eddy_v * eddy_z * cosine], axis=2)
    owned_count = slot_wavenumber.shape[0]
    piece = lax.all_gather(fluxes, "lon", axis=1, tiled=True)
    table = fourier_table(slot_wavenumber, piece.shape[1])
    coeffs = jnp.einsum("jic,iqt->jqtc", piece, table, precision=lax.Precision.HIGHEST)
    present = slot_wavenumber >= 0
    clipped = jnp.maximum(slot_wavenumber, 0)
    scale = (clipped.astype(jnp.float32) / MAXM)[None, :, None]
    cos_u = coeffs[:, :, 0, :S]
    sin_u = coeffs[:, :, 1, :S]
    cos_v = coeffs[:, :, 0, S:]
    sin_v = coeffs[:, :, 1, S:]
    right_p = jnp.concatenate([scale * sin_u, scale * cos_u], axis=2).astype(jnp.bfloat16)
    right_h = jnp.concatenate([-cos_v, sin_v], axis=2).astype(jnp.bfloat16)
    table_p = legendre_p.reshape(band_rows, owned_count, MAXM)
    table_h = legendre_h.reshape(band_rows, owned_count, MAXM)
    partial_sum = jnp.einsum("jqn,jqc->qnc", table_p, right_p, preferred_element_type=jnp.float32)
    partial_sum = partial_sum + jnp.einsum(
        "jqn,jqc->qnc", table_h, right_h, preferred_element_type=jnp.float32
    )
    degree = jnp.arange(MAXM, dtype=jnp.int32)
    keep = ((degree[None, :] >= clipped[:, None]) & present[:, None]).astype(jnp.float32)
    flat_terms = (partial_sum * keep[:, :, None]).reshape(owned_count * MAXM, 2 * S)
    share = flat_terms.shape[0] // lat_count
    summed = lax.psum(flat_terms, "lat")
    mine = lax.dynamic_slice_in_dim(summed, lax.axis_index("lat") * share, share, 0)
    power = mine[:, :S] ** 2 + mine[:, S:] ** 2
    spectra = jnp.dot(power, onehot, precision=lax.Precision.HIGHEST) / DAYS
    return spectra.T


def solution(mesh):
    placed = (
        P("lat", "lon", None),
        P("lat", "lon", None),
        P("lat", "lon", None),
        P(),
        P("lon"),
        P("lat", "lon"),
        P("lat", "lon"),
    )
    return jax.shard_map(
        body, mesh=mesh, in_specs=placed, out_specs=P(None, ("lon", "lat")), check_vma=False
    )
```

profile of v0, /device:TPU:1, one launch (start us, length us, event | category | flops | bytes accessed | tf_op | source)
XLA Modules:
  0.0 525.2 jit_solution(9790209907816465756)
XLA Ops:
  6.5 0.0 copy-start.2
  6.5 0.0 all-gather.2.cloned.1.call-start
  6.6 1.3 fusion.16
  7.9 1.4 convolution_subtract_fusion.1
  9.3 1.2 fusion.15
  10.5 1.2 fusion.17
  11.8 0.0 copy-done
  11.8 1.1 fusion.13
  12.9 0.0 copy-done.2
  12.9 0.0 copy-done.1
  12.9 0.4 fusion.14
  13.3 0.1 pad_maximum_fusion
  13.4 1.7 copy.19
  15.1 0.0 all-gather.2.cloned.1.call-update
  15.1 0.2 all-reduce.2.cloned.1.call-start
  15.3 4.0 reshape.180
  19.3 0.0 copy-start.3
  19.3 4.0 reshape.179
  23.4 0.0 copy-done.3
  23.4 0.1 fusion.37
  23.5 1.4 cosine_multiply_fusion
  24.9 262.6 %all-gather.2.cloned.1.call-done = f32[45,1440,32]{0,2,1:T(8,128)} async-done(((f32[45,45,32]{0,2,1:T(8,128)}), f32[45,1440,32]{0,2,1:T(8,128)}) %all-gather.2.cloned.1.call-update) | async-done | bytes 8294416 | tf_op jit(solution)/shard_map/all_gather | solution.py:44
  287.4 17.4 %copy.20 = f32[45,1440,32]{1,0,2:T(8,128)} copy(f32[45,1440,32]{0,2,1:T(8,128)} %all-gather.2.cloned.1.call-done) | data formatting | bytes 16588800 | tf_op jit(solution)/shard_map/all_gather | solution.py:44
  304.8 18.9 %fusion.8 = f32[45,23,2,32]{0,1,3,2:T(8,128)S(1)} fusion(f32[45,1440,32]{1,0,2:T(8,128)} %copy.20, f32[1440,23,1]{0,1,2:T(8,128)} %get-tuple-element.8, f32[1440,23,1]{0,1,2:T(8,128)S(1)} %get-tuple-element.7), kind=kOutput, calls=%fused_computation.8 | convolution fusion | flops 1144693504 | bytes 8824320 | tf_op jit(solution)/shard_map/jic,iqt->jqtc/dot_general | solution.py:46
  323.7 0.1 fusion.24
  323.9 0.5 fusion.2
  324.4 0.6 multiply_bitcast_fusion
  325.0 1.3 copy.25
  326.3 2.0 reshape.181
  328.3 0.0 all-reduce.2.cloned.1.call-update
  328.4 188.2 %all-reduce.2.cloned.1.call-done = f32[16560,32]{0,1:T(8,128)} async-done(((f32[16560,32]{0,1:T(8,128)}), f32[16560,32]{0,1:T(8,128)}) %all-reduce.2.cloned.1.call-update) | async-done | bytes 2119696 | tf_op jit(solution)/shard_map/psum | solution.py:66
  516.6 1.8 convolution_multiply_fusion
  (10 shorter events, 0.2 us)
Async XLA Ops:
  6.5 6.3 %copy-start.2 = (s32[16]{0:T(128)S(1)}, s32[16]{0:T(128)}, u32[]{:S(2)}) copy-start(s32[16]{0:T(128)} %param.10) | copy-start | bytes 196
  6.5 5.3 %copy-start = (f32[45,45,16]{1,2,0:T(8,128)S(1)}, f32[45,45,16]{1,2,0:T(8,128)}, u32[]{:S(2)}) copy-start(f32[45,45,16]{1,2,0:T(8,128)} %param.8) | copy-start | bytes 388804
  6.5 6.3 %copy-start.1 = (f32[45,45,16]{1,2,0:T(8,128)S(1)}, f32[45,45,16]{1,2,0:T(8,128)}, u32[]{:S(2)}) copy-start(f32[45,45,16]{1,2,0:T(8,128)} %param.7) | copy-start | bytes 388804
  6.5 280.9 %all-gather.2.cloned.1.call-start = ((), (), s32[]{:S(2)}) async-start(), calls=%async_computation | async-start | bytes 24330240 | tf_op jit(solution)/shard_map/all_gather | solution.py:44
  15.1 501.5 %all-reduce.2.cloned.1.call-start = ((), (), s32[]{:S(2)}) async-start(), calls=%async_computation.1 | async-start | bytes 4259840 | tf_op jit(solution)/shard_map/psum | solution.py:66
  19.3 4.0 copy-start.3
Sparse Core Ops, SparseCore 0:
  15.2 272.1 all-gather.1
  328.5 188.0 all-reduce.1
where the time goes:
time: 526 us; the launch traced here: 525 us
  waiting for transfers between devices  451 us (86%)
  local copies, waits for them, and re-layouts  30.4 us (6%)
  matrix products  28.3 us (5%)
  between operations  13.6 us (3%)
    all_gather x1, waiting for transfers between devices, body(): piece = lax.all_gather(fluxes, 'lon', axis=1, tiled=True)  263 us
    psum x1, waiting for transfers between devices, body(): summed = lax.psum(flat_terms, 'lat')  188 us
    dot_general x1, matrix products, body(): jnp.einsum('jic,iqt->jqtc', piece, table, precision=lax.Precision.HIGHEST)  18.9 us
    all_gather x1, local copies, waits for them, and re-layouts, body(): piece = lax.all_gather(fluxes, 'lon', axis=1, tiled=True)  17.4 us
  transfers between devices with their start and end apart: 2, of which 2 were waited for; matrix products, arithmetic and copies ran while one was open for 2% of the time, Pallas kernels for 0%

commit v1 on v0

--- a/solution.py
+++ b/solution.py
@@ -41,7 +41,10 @@
     cosine = jnp.cos(latitude)[:, None, None]
     fluxes = jnp.concatenate([eddy_u * eddy_z * cosine, eddy_v * eddy_z * cosine], axis=2)
     owned_count = slot_wavenumber.shape[0]
-    piece = lax.all_gather(fluxes, "lon", axis=1, tiled=True)
+    count_2 = lax.axis_size("lon")
+    tiles = jnp.stack([fluxes for _ in range(count_2)])
+    tiles = lax.all_to_all(tiles, "lon", split_axis=0, concat_axis=0)
+    piece = jnp.concatenate(tiles, axis=1)
     table = fourier_table(slot_wavenumber, piece.shape[1])
     coeffs = jnp.einsum("jic,iqt->jqtc", piece, table, precision=lax.Precision.HIGHEST)
     present = slot_wavenumber >= 0

time: 526 us -> 662 us (1.26)
  local copies, waits for them, and re-layouts: 30.4 us -> 163 us
  waiting for transfers between devices: 451 us -> 414 us
  other arithmetic: 1.8 us -> 28.1 us
  starting transfers between devices: 0.22 us -> 13.9 us
    all_gather x1 -> x0, waiting for transfers between devices: 263 us -> none  [body(): piece = lax.all_gather(fluxes, 'lon', axis=1, tiled=True)]
    all_to_all x0 -> x1, waiting for transfers between devices: none -> 205 us  [body(): tiles = lax.all_to_all(tiles, 'lon', split_axis=0, concat_axis=0)]
    unnamed x8 -> x13, local copies, waits for them, and re-layouts: 0.02 us -> 93.2 us
    reshape x0 -> x3, local copies, waits for them, and re-layouts: none -> 59.2 us  [body(): piece = jnp.concatenate(tiles, axis=1)]
    all_to_all x0 -> x1, other arithmetic: none -> 26.3 us  [body(): tiles = lax.all_to_all(tiles, 'lon', split_axis=0, concat_axis=0)]
    psum x1, waiting for transfers between devices: 188 us -> 209 us  [body(): summed = lax.psum(flat_terms, 'lat')]
    all_gather x1 -> x0, local copies, waits for them, and re-layouts: 17.4 us -> none  [body(): piece = lax.all_gather(fluxes, 'lon', axis=1, tiled=True)]
    all_to_all x0 -> x1, starting transfers between devices: none -> 13.7 us  [body(): tiles = lax.all_to_all(tiles, 'lon', split_axis=0, concat_axis=0)]
  transfers between devices with their start and end apart: 2 -> 2, of which waited for: 2 -> 2; matrix products, arithmetic and copies ran while one was open for 2% -> 1% of each run, Pallas kernels for 0% -> 0%
where the time goes in v1:
time: 662 us; the launch traced here: 661 us
  waiting for transfers between devices  414 us (63%)
  local copies, waits for them, and re-layouts  163 us (25%)
  other arithmetic  28.1 us (4%)
  matrix products  28.1 us (4%)
  starting transfers between devices  13.9 us (2%)
  between operations  13.6 us (2%)
    psum x1, waiting for transfers between devices, body(): summed = lax.psum(flat_terms, 'lat')  209 us
    all_to_all x1, waiting for transfers between devices, body(): tiles = lax.all_to_all(tiles, 'lon', split_axis=0, concat_axis=0)  205 us
    unnamed x13, local copies, waits for them, and re-layouts  93.2 us
    reshape x3, local copies, waits for them, and re-layouts, body(): piece = jnp.concatenate(tiles, axis=1)  59.2 us
    all_to_all x1, other arithmetic, body(): tiles = lax.all_to_all(tiles, 'lon', split_axis=0, concat_axis=0)  26.3 us
    dot_general x1, matrix products, body(): jnp.einsum('jic,iqt->jqtc', piece, table, precision=lax.Precision.HIGHEST)  18.6 us
    all_to_all x1, starting transfers between devices, body(): tiles = lax.all_to_all(tiles, 'lon', split_axis=0, concat_axis=0)  13.7 us
  transfers between devices with their start and end apart: 2, of which 2 were waited for; matrix products, arithmetic and copies ran while one was open for 1% of the time, Pallas kernels for 0%

profile of v1, /device:TPU:1, one launch (start us, length us, event | category | flops | bytes accessed | tf_op | source)
XLA Modules:
  0.0 660.6 jit_solution(3371074014837616427)
XLA Ops:
  6.6 1.3 fusion.11
  7.9 1.4 convolution_subtract_fusion.1
  9.3 1.2 fusion.10
  10.5 1.2 fusion.12
  11.8 1.1 fusion.8
  12.9 0.4 fusion.9
  13.3 0.1 pad_maximum_fusion
  13.4 10.9 %broadcast_bitcast_fusion = f32[32,45,32,45]{3,2,1,0:T(8,128)} fusion(f32[45,45,32]{1,2,0:T(8,128)S(1)} %pad_maximum_fusion), kind=kLoop, calls=%fused_computation.76 | loop fusion | bytes 8553600
  24.2 34.5 %reshape.197 = f32[32,1,64800]{2,1,0:T(1,128)} reshape(f32[32,45,32,45]{3,2,1,0:T(8,128)} %broadcast_bitcast_fusion) | data formatting | bytes 16588800
  58.8 13.7 %all-to-all-start = ((f32[32,1,64800]{2,1,0:T(1,128)}), f32[32,1,64800]{2,1,0:T(1,128)}, u32[]{:S(2)}, u32[]{:S(2)}) async-start(f32[32,1,64800]{2,1,0:T(1,128)} %reshape.197), calls=%async_computation | async-start | bytes 16613376 | tf_op jit(solution)/shard_map/all_to_all | solution.py:46
  72.5 0.2 all-reduce.2.cloned.1.call-start
  72.7 2.9 reshape.190
  75.6 0.0 copy-start.4
  75.6 4.0 reshape.189
  79.7 0.1 fusion.32
  79.8 1.4 cosine_multiply_fusion
  81.1 204.7 %all-to-all-done = f32[32,1,64800]{2,1,0:T(1,128)} async-done(((f32[32,1,64800]{2,1,0:T(1,128)}), f32[32,1,64800]{2,1,0:T(1,128)}, u32[]{:S(2)}, u32[]{:S(2)}) %all-to-all-start) | async-done | bytes 8294432 | tf_op jit(solution)/shard_map/all_to_all | solution.py:46
  285.8 0.5 broadcast.216
  286.3 26.3 %reduce = f32[32,64800]{1,0:T(8,128)} reduce(f32[32,1,64800]{2,1,0:T(1,128)} %all-to-all-done, f32[]{:T(128)} %broadcast.216), dimensions={1}, to_apply=%all_to_all.3.reduce_sub_computation | reduce | bytes 16588804 | tf_op jit(solution)/shard_map/all_to_all | solution.py:46
  312.6 47.8 %reshape.198 = f32[32,45,32,45]{3,2,1,0:T(8,128)} reshape(f32[32,64800]{1,0:T(8,128)} %reduce) | data formatting | bytes 16588800
  360.4 9.4 %bitcast_bitcast_fusion = f32[45,32,45,32]{2,3,0,1:T(8,128)S(1)} fusion(f32[32,45,32,45]{3,2,1,0:T(8,128)} %reshape.198), kind=kLoop, calls=%fused_computation.75 | loop fusion | bytes 16588800 | tf_op jit(solution)/shard_map/reshape | solution.py:47
  369.8 28.3 %copy.27 = f32[45,32,45,32]{2,1,0,3:T(8,128)} copy(f32[45,32,45,32]{2,3,0,1:T(8,128)S(1)} %bitcast_bitcast_fusion) | data formatting | bytes 16588800 | tf_op jit(solution)/shard_map/reshape | solution.py:47
  398.1 21.5 %reshape.194 = f32[45,1440,32,1]{1,0,2,3:T(8,128)} reshape(f32[45,32,45,32]{2,1,0,3:T(8,128)} %copy.27) | data formatting | bytes 16588800 | tf_op jit(solution)/shard_map/reshape | solution.py:47
  419.6 18.6 %convolution_bitcast_fusion = f32[45,23,2,32]{0,1,3,2:T(8,128)S(1)} fusion(f32[45,1440,32,1]{1,0,2,3:T(8,128)} %reshape.194, f32[1440,23,1]{0,1,2:T(8,128)} %get-tuple-element.8, f32[1440,23,1]{0,1,2:T(8,128)S(1)} %get-tuple-element.7), kind=kOutput, calls=%fused_computation.6 | convolution fusion | flops 1144693504 | bytes 8824320 | tf_op jit(solution)/shard_map/jic,iqt->jqtc/dot_general | solution.py:49
  438.3 0.1 fusion.19
  438.5 0.5 fusion
  439.0 0.6 multiply_bitcast_fusion
  439.6 1.3 copy.25
  441.0 2.0 reshape.191
  443.0 0.0 all-reduce.2.cloned.1.call-update
  443.0 209.0 %all-reduce.2.cloned.1.call-done = f32[16560,32]{0,1:T(8,128)} async-done(((f32[16560,32]{0,1:T(8,128)}), f32[16560,32]{0,1:T(8,128)}) %all-reduce.2.cloned.1.call-update) | async-done | bytes 2119696 | tf_op jit(solution)/shard_map/psum | solution.py:69
  652.0 1.8 convolution_multiply_fusion
  (17 shorter events, 0.2 us)
Async XLA Ops:
  6.5 6.3 copy-start.3
  6.5 5.3 copy-start.1
  6.5 6.3 copy-start.2
  58.8 13.9 %copy-start = (bf16[45,16560]{1,0:T(8,128)(2,1)S(1)}, bf16[45,16560]{1,0:T(8,128)(2,1)}, u32[]{:S(2)}) copy-start(bf16[45,16560]{1,0:T(8,128)(2,1)} %param.13) | copy-start | bytes 4471204
  58.8 227.0 %all-to-all-start = ((f32[32,1,64800]{2,1,0:T(1,128)}), f32[32,1,64800]{2,1,0:T(1,128)}, u32[]{:S(2)}, u32[]{:S(2)}) async-start(f32[32,1,64800]{2,1,0:T(1,128)} %reshape.197), calls=%async_computation | async-start | bytes 16613376 | tf_op jit(solution)/shard_map/all_to_all | solution.py:46
  72.5 579.5 %all-reduce.2.cloned.1.call-start = ((), (), s32[]{:S(2)}) async-start(), calls=%async_computation.1 | async-start | bytes 4259840 | tf_op jit(solution)/shard_map/psum | solution.py:69
  75.6 4.0 copy-start.4
Sparse Core Ops, SparseCore 0:
  443.1 208.8 all-reduce.1
